TPU v7x, 512 devices: a whole 4x8x8 slice. The times are simulated.
512 devices in a mesh: ka: 8 (over y_hi, core), pb: 16 (over y_lo, z), row: 4 (over x).
Axes of the slice: x: 4, y: 8 (y_hi: 4, y_lo: 2; y = y_hi * 2 + y_lo), z: 8, core: 2. Of those that a mesh axis runs over, the one named last changes fastest.
Arguments:
- coupling: bfloat16 [64, 64, 20736], P('pb', ('ka', 'row')), may hold values from -1 to 1
- rotation: bfloat16 [64, 36, 36], P('pb'), may hold values from -1 to 1
- freq: float32 [64, 36], P('pb'), may hold values from 0.02 to 0.3
- eigvec: bfloat16 [1024, 24, 24], P(('ka', 'row')), may hold values from -1.25 to 1.25
- energies: float32 [1024, 24], P(('ka', 'row')), may hold values from -1.5 to 1.5
- window: int32 [1024], P(('ka', 'row')), may hold values from 12 to 24
- kq_index: int32 [64, 1024], P('pb'), may hold values from 0 to 1023, as said below
- kpoints: float32 [1024, 3], replicated, may hold values from 0 to 1
- lattice: int32 [64, 3], replicated, may hold values from -3 to 3
Outputs:
- electron: float32 [1024, 24], P(('ka', 'row'))
- phonon: float32 [64, 36], P('pb')
Inputs may be any that keep to these rules, and one draw needn't show every extreme that they name: The k-points form a shifted grid of 1024 points, (1024 // 64) x 8 x 8, listed in an order drawn from the seed; each q-point is a vector of that grid without the shift. kq_index[q, k] is the index of the k-point equal to kpoints[k] plus the q-point's vector modulo 1, so each row of kq_index is a permutation of 0 to 1023.
All inputs are finite; a program needn't handle non-finite values.
Results may differ from a plain program's by a relative error of at most 0.00089.
Values may be sent and summed in bfloat16 or wider, within the bound.
A program may use at most 128 MiB of HBM per device.

v0:
```python
import math
import jax
import jax.numpy as jnp
from jax import lax
from jax.sharding import PartitionSpec as P

SIGMA = 0.1
THERMAL_ENERGY_KT = 0.2


def phase_table(lattice, kpoint_rows):
    rvec = lattice.astype(jnp.float32)
    argument = (
        rvec[:, 0:1] * kpoint_rows[:, 0][None, :]
        + rvec[:, 1:2] * kpoint_rows[:, 1][None, :]
        + rvec[:, 2:3] * kpoint_rows[:, 2][None, :]
    )
    return jnp.cos(2.0 * math.pi * argument).astype(jnp.bfloat16)


def block_terms(
    coup_rows, phase_cols, rot_rows, freq_rows, eig_k, eig_kq, level_k, level_kq, lim_k, lim_kq
):
    q_block = coup_rows.shape[0]
    k_block = phase_cols.shape[1]
    columns = q_block * k_block
    n_modes = rot_rows.shape[1]
    n_bands = eig_k.shape[0]
    norm = 1.0 / (math.sqrt(2.0 * math.pi) * SIGMA)
    bloch = jnp.einsum(
        "qrf,rk->fqk", coup_rows, phase_cols, preferred_element_type=jnp.float32
    ).astype(jnp.bfloat16)
    bloch = bloch.reshape(n_modes, n_bands, n_bands, columns)
    rot_cols = jnp.repeat(jnp.transpose(rot_rows, (1, 2, 0)), k_block, axis=2)
    modal = jnp.einsum(
        "amnc,abc->bmnc", bloch, rot_cols, preferred_element_type=jnp.float32
    ).astype(jnp.bfloat16)
    eig_k_cols = jnp.tile(eig_k, (1, 1, q_block))
    right = jnp.einsum(
        "bmjc,jnc->bmnc", modal, eig_k_cols, preferred_element_type=jnp.float32
    ).astype(jnp.bfloat16)
    coupled = jnp.einsum("imc,binc->bmnc", eig_kq, right, preferred_element_type=jnp.float32)
    level_k_cols = jnp.tile(level_k, (1, q_block))
    lim_k_cols = jnp.tile(lim_k, (q_block,))
    freq_cols = jnp.repeat(freq_rows.T, k_block, axis=1)
    diff = level_kq[None, :, None, :] - level_k_cols[None, None, :, :] - freq_cols[:, None, None, :]
    delta = jnp.exp(-(diff * diff) / (2.0 * SIGMA * SIGMA)) * norm
    bands = jnp.arange(n_bands).astype(jnp.float32)
    mask_m = (bands[:, None] < lim_kq[None, :]).astype(jnp.float32)
    mask_n = (bands[:, None] < lim_k_cols[None, :]).astype(jnp.float32)
    strength = coupled * coupled * delta * mask_m[None, :, None, :] * mask_n[None, None, :, :]
    filling_initial = jax.nn.sigmoid(-level_k_cols / THERMAL_ENERGY_KT)
    filling_final = jax.nn.sigmoid(-level_kq / THERMAL_ENERGY_KT)
    elec = jnp.sum(strength, axis=(0, 1)).reshape(n_bands, q_block, k_block).sum(axis=1)
    phon = jnp.sum(
        strength * (filling_initial[None, None, :, :] - filling_final[None, :, None, :]),
        axis=(1, 2),
    )
    phon = phon.reshape(n_modes, q_block, k_block).sum(axis=2)
    return (elec, phon)


def on_device(coupling, rotation, freq, eigvec, energies, window, kq_index, kpoints, lattice):
    n_ka = lax.axis_size("ka")
    n_row = lax.axis_size("row")
    n_pb = lax.axis_size("pb")
    k_dev = eigvec.shape[0]
    q_dev = rotation.shape[0]
    n_bands = eigvec.shape[1]
    n_modes = rotation.shape[1]
    total_k = k_dev * n_ka * n_row
    total_q = q_dev * n_pb
    eigen_grid = lax.all_gather(eigvec, ("ka", "row"), axis=0, tiled=True)
    level_all, limit_all = (
        lax.all_gather(energies, ("ka", "row"), axis=0, tiled=True),
        lax.all_gather(window.astype(jnp.float32), ("ka", "row"), axis=0, tiled=True),
    )
    eig_cols = jnp.transpose(eigen_grid, (1, 2, 0))
    level_cols = level_all.T
    ka_pos = lax.axis_index("ka")
    row_pos = lax.axis_index("row")
    coup_full = lax.all_gather(coupling, ("ka", "row"), axis=1, tiled=True)
    q_start = jnp.int32(0)
    k_start = (ka_pos * n_row + row_pos) * k_dev
    kq_mine = lax.dynamic_slice(kq_index, (q_start, k_start), (q_dev, k_dev))
    kp_mine = lax.dynamic_slice(kpoints, (k_start, jnp.int32(0)), (k_dev, 3))
    eig_mine = lax.dynamic_slice_in_dim(eig_cols, k_start, k_dev, 2)
    lev_mine = lax.dynamic_slice_in_dim(level_cols, k_start, k_dev, 1)
    lim_mine = lax.dynamic_slice_in_dim(limit_all, k_start, k_dev, 0)
    phase_all = phase_table(lattice, kp_mine)
    k_block = min(k_dev, 128)
    elec_cols = [None] * (k_dev // k_block)
    index = kq_mine.reshape(-1)
    eig_kq = jnp.take(eig_cols, index, axis=2)
    level_kq = jnp.take(level_cols, index, axis=1)
    lim_kq = jnp.take(limit_all, index, axis=0)
    elec, phon = block_terms(
        coup_full, phase_all, rotation, freq, eig_mine, eig_kq, lev_mine, level_kq, lim_mine, lim_kq
    )
    elec_cols[0] = elec
    elec_local = elec_cols[0].T * (1.0 / (total_q * n_modes * n_bands))
    phon_local = phon.T * (1.0 / (total_k * n_bands))
    phonon = lax.psum(phon_local, ("ka", "row"))
    electron = lax.psum(elec_local, "pb")
    return (electron, phonon)


def solution(mesh):
    return jax.shard_map(
        on_device,
        mesh=mesh,
        in_specs=(
            P("pb", ("ka", "row"), None),
            P("pb", None, None),
            P("pb", None),
            P(("ka", "row"), None, None),
            P(("ka", "row"), None),
            P(("ka", "row")),
            P("pb", None),
            P(),
            P(),
        ),
        out_specs=(P(("ka", "row"), None), P("pb", None)),
        check_vma=False,
    )
```

profile of v0, /device:TPU:40, one launch (start us, length us, event | category | flops | bytes accessed | tf_op | source)
XLA Modules:
  0.0 554.0 jit_solution(66930285304489676)
XLA Ops:
  7.2 0.0 copy-start
  7.2 0.0 all-gather.4.cloned.1.call-start
  7.2 1.7 copy.47
  9.0 0.0 all-gather.4.cloned.1.call-update
  9.0 0.0 all-gather.6.cloned.1.call-start
  9.0 1.8 copy.49
  10.9 0.0 all-gather.6.cloned.1.call-update
  10.9 0.0 copy-done
  10.9 0.1 constant_dynamic-slice_fusion
  11.0 0.1 reshape.215
  11.1 0.1 reshape.214
  11.2 0.7 convert_element_type.50
  11.8 1.3 dynamic-slice.8
  13.8 0.8 convert_dynamic-update-slice_fusion
  14.5 78.9 %all-reduce = f32[1024]{0:T(1024)S(1)} all-reduce(f32[1024]{0:T(1024)S(1)} %convert_dynamic-update-slice_fusion), channel_id=1, replica_groups=mesh['ka'=8,'pb'=16,'row'=4] {'ka','row'}, use_global_device_ids=true, to_apply=%add | all-reduce | flops 1024 | bytes 8192
  93.5 0.1 dynamic_slice.19
  93.6 1.0 gather_fusion.2
  94.6 0.1 lt.84
  94.6 0.8 copy.79
  95.4 0.1 compare_convert_fusion.1
  95.5 0.1 copy.62
  95.6 0.1 copy.63
  95.7 82.7 %all-gather = f32[32,32,24]{1,2,0:T(8,128)S(1)} all-gather(f32[1,32,24]{1,2,0:T(8,128)} %bitcast.93), channel_id=1, replica_groups=mesh['ka'=8,'pb'=16,'row'=4] {'ka','row'}, dimensions={0}, use_global_device_ids=true | all-gather | bytes 101376 | tf_op jit(solution)/shard_map/all_gather | solution.py:75
  178.4 0.2 copy.57
  178.6 0.1 copy.60
  178.7 0.1 tile.13
  178.8 0.1 copy.61
  178.9 0.1 copy.64
  179.0 0.7 gather_fusion.1
  179.7 0.1 copy.58
  179.8 0.1 copy.65
  179.9 0.1 copy.59
  180.0 0.8 constant_dynamic-slice_fusion.1
  180.8 2.2 broadcast_subtract_fusion
  182.9 0.0 all-gather.4.cloned.1.call-done
  182.9 0.9 dynamic-slice_bitcast_fusion
  183.9 0.1 copy.48
  184.0 3.5 gather_fusion
  187.5 0.0 all-gather.6.cloned.1.call-done
  187.6 8.0 %fusion.4 = bf16[20736,4,32]{0,2,1:T(8,128)(2,1)} fusion(bf16[4,64,20736]{2,0,1:T(4,128)(2,1)} %all-gather.6.cloned.1.call-done, f32[32]{0:T(128)S(1)} %get-tuple-element.18, f32[64]{0:T(128)S(1)} %get-tuple-element.15, f32[32]{0:T(128)S(1)} %get-tuple-element.19, f32[64]{0:T(128)S(1)} %get-tuple-element.16, f32[32]{0:T(128)S(1)} %get-tuple-element.17, ...), kind=kOutput, calls=%fused_computation.10 | convolution fusion | flops 342407168 | bytes 15926400 | tf_op jit(solution)/shard_map/qrf,rk->fqk/dot_general | solution.py:30
  195.6 47.2 %reshape.253 = bf16[36,24,24,128]{2,1,0,3:T(8,128)(2,1)} reshape(bf16[20736,4,32]{0,2,1:T(8,128)(2,1)} %fusion.4) | data formatting | bytes 10616832 | tf_op jit(solution)/shard_map/reshape | solution.py:33
  242.8 0.1 tile.10
  242.9 0.2 broadcast_in_dim.40.clone
  243.1 0.0 copy-start.2
  243.1 23.0 %convert_bitcast_fusion = bf16[36,24,24,128]{0,2,1,3:T(8,128)(2,1)} fusion(bf16[24,24,128,1]{0,1,3,2:T(8,128)(2,1)S(1)} %bitcast.86, bf16[36,36,128,1]{1,0,3,2:T(8,128)(2,1)S(1)} %bitcast.85, bf16[36,24,24,128]{2,1,0,3:T(8,128)(2,1)} %reshape.253), kind=kOutput, calls=%fused_computation.15 | convolution fusion | flops 323813376 | bytes 11096064 | tf_op jit(solution)/shard_map/bmjc,jnc->bmnc/dot_general | solution.py:39
  266.1 0.0 copy-done.2
  266.1 0.0 copy-start.1
  266.1 69.3 %multiply_reduce_fusion = (f32[36,128]{0,1:T(8,128)S(1)}, f32[24,128]{0,1:T(8,128)S(1)}) fusion(f32[24,24,128]{0,1,2:T(8,128)} %get-tuple-element.22, f32[24,128]{0,1:T(8,128)S(1)} %copy.63, f32[24,128]{0,1:T(8,128)S(1)} %copy.62, f32[36,128]{0,1:T(8,128)S(1)} %bitcast.90, f32[24,24,128]{0,1,2:T(8,128)} %get-tuple-element.23, ...), kind=kOutput, calls=%fused_computation.6 | convolution fusion | flops 159318528 | bytes 6119552 | tf_op jit(solution)/shard_map/imc,binc->bmnc/dot_general | solution.py:42
  335.5 69.8 %psum.14 = f32[32,24]{1,0:T(8,128)S(1)} all-reduce(f32[32,24]{1,0:T(8,128)S(1)} %multiply_bitcast_fusion.1), channel_id=1, replica_groups=mesh['ka'=8,'pb'=16,'row'=4] {'pb'}, use_global_device_ids=true, to_apply=%region_2.3 | all-reduce | flops 768 | bytes 6144 | tf_op jit(solution)/shard_map/psum | solution.py:104
  405.3 0.7 copy.67
  405.9 0.1 copy.78
  406.0 140.5 %psum.15 = f32[4,36]{0,1:T(8,128)S(1)} all-reduce(f32[4,36]{0,1:T(8,128)S(1)} %multiply_bitcast_fusion), channel_id=1, replica_groups=mesh['ka'=8,'pb'=16,'row'=4] {'ka','row'}, use_global_device_ids=true, to_apply=%region_5.6 | all-reduce | flops 144 | bytes 1152 | tf_op jit(solution)/shard_map/psum | solution.py:103
  546.5 0.7 copy.68
  547.2 0.0 copy-done.1
  (17 shorter events, 0.2 us)
Async XLA Ops:
  7.2 3.7 copy-start
  7.2 175.7 %all-gather.4.cloned.1.call-start = ((), (), s32[]{:S(2)}) async-start(), calls=%async_computation | async-start | bytes 6488064 | tf_op jit(solution)/shard_map/all_gather | solution.py:73
  9.0 178.6 %all-gather.6.cloned.1.call-start = ((), (), s32[]{:S(2)}) async-start(), calls=%async_computation.1 | async-start | bytes 10948608 | tf_op jit(solution)/shard_map/all_gather | solution.py:82
  243.1 23.0 %copy-start.2 = (f32[4,36]{1,0:T(4,128)S(1)}, f32[4,36]{1,0:T(4,128)}, u32[]{:S(2)}) copy-start(f32[4,36]{1,0:T(4,128)} %param.11) | copy-start | bytes 1732
  266.1 281.1 %copy-start.1 = (s32[4,1024]{1,0:T(4,128)S(1)}, s32[4,1024]{1,0:T(4,128)}, u32[]{:S(2)}) copy-start(s32[4,1024]{1,0:T(4,128)} %param.15) | copy-start | bytes 49156
Sparse Core Ops, SparseCore 0:
  11.1 75.5 all-gather.3
  89.9 93.6 all-gather.5
where the time goes:
time: 555 us; the launch traced here: 554 us
  blocking collectives  372 us (67%)
  matrix products  100 us (18%)
  local copies, waits for them, and re-layouts  63 us (11%)
  between operations  14.9 us (3%)
    psum x1, blocking collectives, on_device(): phonon = lax.psum(phon_local, ('ka', 'row'))  140 us
    all_gather x1, blocking collectives, on_device(): lax.all_gather(energies, ('ka', 'row'), axis=0, tiled=True)  82.7 us
    unnamed x1, blocking collectives  78.9 us
    psum x1, blocking collectives, on_device(): electron = lax.psum(elec_local, 'pb')  69.8 us
    dot_general x1, matrix products, block_terms(): jnp.einsum('imc,binc->bmnc', eig_kq, right, preferred_element_type=jnp.fl...  69.3 us
    reshape x1, local copies, waits for them, and re-layouts, block_terms(): bloch = bloch.reshape(n_modes, n_bands, n_bands, columns)  47.2 us
    dot_general x1, matrix products, block_terms(): jnp.einsum('bmjc,jnc->bmnc', modal, eig_k_cols, preferred_element_type=jn...  23 us
  transfers between devices with their start and end apart: 2, of which 0 were waited for; matrix products, arithmetic and copies ran while one was open for 3% of the time, Pallas kernels for 0%

commit v1 on v0

--- a/solution.py
+++ b/solution.py
@@ -100,7 +100,7 @@
     elec_cols[0] = elec
     elec_local = elec_cols[0].T * (1.0 / (total_q * n_modes * n_bands))
     phon_local = phon.T * (1.0 / (total_k * n_bands))
-    phonon = lax.psum(phon_local, ("ka", "row"))
+    phonon = lax.psum(lax.psum(phon_local, "ka"), "row")
     electron = lax.psum(elec_local, "pb")
     return (electron, phonon)
 

time: 555 us -> 458 us (0.83)
  blocking collectives: 372 us -> 275 us
    psum x1 -> x2, blocking collectives: 140 us -> 43.7 us  [on_device(): phonon = lax.psum(lax.psum(phon_local, 'ka'), 'row')]
  transfers between devices with their start and end apart: 2 -> 2, of which waited for: 0 -> 0; matrix products, arithmetic and copies ran while one was open for 3% -> 4% of each run, Pallas kernels for 0% -> 0%
where the time goes in v1:
time: 458 us; the launch traced here: 457 us
  blocking collectives  275 us (60%)
  matrix products  100 us (22%)
  local copies, waits for them, and re-layouts  63.1 us (14%)
  between operations  14.9 us (3%)
    all_gather x1, blocking collectives, on_device(): lax.all_gather(energies, ('ka', 'row'), axis=0, tiled=True)  82.7 us
    unnamed x1, blocking collectives  78.9 us
    psum x1, blocking collectives, on_device(): electron = lax.psum(elec_local, 'pb')  69.8 us
    dot_general x1, matrix products, block_terms(): jnp.einsum('imc,binc->bmnc', eig_kq, right, preferred_element_type=jnp.fl...  69.3 us
    reshape x1, local copies, waits for them, and re-layouts, block_terms(): bloch = bloch.reshape(n_modes, n_bands, n_bands, columns)  47.2 us
    psum x2, blocking collectives, on_device(): phonon = lax.psum(lax.psum(phon_local, 'ka'), 'row')  43.7 us
    dot_general x1, matrix products, block_terms(): jnp.einsum('bmjc,jnc->bmnc', modal, eig_k_cols, preferred_element_type=jn...  23 us
  transfers between devices with their start and end apart: 2, of which 0 were waited for; matrix products, arithmetic and copies ran while one was open for 4% of the time, Pallas kernels for 0%

profile of v1, /device:TPU:40, one launch (start us, length us, event | category | flops | bytes accessed | tf_op | source)
XLA Modules:
  0.0 457.2 jit_solution(8716118293926351780)
XLA Ops:
  7.2 0.0 copy-start
  7.2 0.0 all-gather.4.cloned.1.call-start
  7.2 1.7 copy.47
  9.0 0.0 all-gather.4.cloned.1.call-update
  9.0 0.0 all-gather.6.cloned.1.call-start
  9.0 1.8 copy.49
  10.9 0.0 all-gather.6.cloned.1.call-update
  10.9 0.0 copy-done
  10.9 0.1 constant_dynamic-slice_fusion
  11.0 0.1 reshape.215
  11.1 0.1 reshape.214
  11.2 0.7 convert_element_type.50
  11.8 1.3 dynamic-slice.8
  13.8 0.8 convert_dynamic-update-slice_fusion
  14.5 78.9 %all-reduce = f32[1024]{0:T(1024)S(1)} all-reduce(f32[1024]{0:T(1024)S(1)} %convert_dynamic-update-slice_fusion), channel_id=1, replica_groups=mesh['ka'=8,'pb'=16,'row'=4] {'ka','row'}, use_global_device_ids=true, to_apply=%add | all-reduce | flops 1024 | bytes 8192
  93.5 0.1 dynamic_slice.19
  93.6 1.0 gather_fusion.2
  94.6 0.1 lt.84
  94.6 0.8 copy.79
  95.4 0.1 compare_convert_fusion.1
  95.5 0.1 copy.62
  95.6 0.1 copy.63
  95.7 82.7 %all-gather = f32[32,32,24]{1,2,0:T(8,128)S(1)} all-gather(f32[1,32,24]{1,2,0:T(8,128)} %bitcast.93), channel_id=1, replica_groups=mesh['ka'=8,'pb'=16,'row'=4] {'ka','row'}, dimensions={0}, use_global_device_ids=true | all-gather | bytes 101376 | tf_op jit(solution)/shard_map/all_gather | solution.py:75
  178.4 0.2 copy.57
  178.6 0.1 copy.60
  178.7 0.1 tile.13
  178.8 0.1 copy.61
  178.9 0.1 copy.64
  179.0 0.7 gather_fusion.1
  179.7 0.1 copy.58
  179.8 0.1 copy.65
  179.9 0.1 copy.59
  180.0 0.8 constant_dynamic-slice_fusion.1
  180.8 2.2 broadcast_subtract_fusion
  182.9 0.0 all-gather.4.cloned.1.call-done
  182.9 0.9 dynamic-slice_bitcast_fusion
  183.9 0.1 copy.48
  184.0 3.5 gather_fusion
  187.5 0.0 all-gather.6.cloned.1.call-done
  187.6 8.0 %fusion.4 = bf16[20736,4,32]{0,2,1:T(8,128)(2,1)} fusion(bf16[4,64,20736]{2,0,1:T(4,128)(2,1)} %all-gather.6.cloned.1.call-done, f32[32]{0:T(128)S(1)} %get-tuple-element.18, f32[64]{0:T(128)S(1)} %get-tuple-element.15, f32[32]{0:T(128)S(1)} %get-tuple-element.19, f32[64]{0:T(128)S(1)} %get-tuple-element.16, f32[32]{0:T(128)S(1)} %get-tuple-element.17, ...), kind=kOutput, calls=%fused_computation.10 | convolution fusion | flops 342407168 | bytes 15926400 | tf_op jit(solution)/shard_map/qrf,rk->fqk/dot_general | solution.py:30
  195.6 47.2 %reshape.253 = bf16[36,24,24,128]{2,1,0,3:T(8,128)(2,1)} reshape(bf16[20736,4,32]{0,2,1:T(8,128)(2,1)} %fusion.4) | data formatting | bytes 10616832 | tf_op jit(solution)/shard_map/reshape | solution.py:33
  242.8 0.1 tile.10
  242.9 0.2 broadcast_in_dim.40.clone
  243.1 0.0 copy-start.2
  243.1 23.0 %convert_bitcast_fusion = bf16[36,24,24,128]{0,2,1,3:T(8,128)(2,1)} fusion(bf16[24,24,128,1]{0,1,3,2:T(8,128)(2,1)S(1)} %bitcast.86, bf16[36,36,128,1]{1,0,3,2:T(8,128)(2,1)S(1)} %bitcast.85, bf16[36,24,24,128]{2,1,0,3:T(8,128)(2,1)} %reshape.253), kind=kOutput, calls=%fused_computation.15 | convolution fusion | flops 323813376 | bytes 11096064 | tf_op jit(solution)/shard_map/bmjc,jnc->bmnc/dot_general | solution.py:39
  266.1 0.0 copy-done.2
  266.1 0.0 copy-start.1
  266.1 69.3 %multiply_reduce_fusion = (f32[36,128]{0,1:T(8,128)S(1)}, f32[24,128]{0,1:T(8,128)S(1)}) fusion(f32[24,24,128]{0,1,2:T(8,128)} %get-tuple-element.22, f32[24,128]{0,1:T(8,128)S(1)} %copy.63, f32[24,128]{0,1:T(8,128)S(1)} %copy.62, f32[36,128]{0,1:T(8,128)S(1)} %bitcast.90, f32[24,24,128]{0,1,2:T(8,128)} %get-tuple-element.23, ...), kind=kOutput, calls=%fused_computation.6 | convolution fusion | flops 159318528 | bytes 6119552 | tf_op jit(solution)/shard_map/imc,binc->bmnc/dot_general | solution.py:42
  335.5 69.8 %psum.21 = f32[32,24]{1,0:T(8,128)S(1)} all-reduce(f32[32,24]{1,0:T(8,128)S(1)} %multiply_bitcast_fusion.1), channel_id=1, replica_groups=mesh['ka'=8,'pb'=16,'row'=4] {'pb'}, use_global_device_ids=true, to_apply=%region_2.3 | all-reduce | flops 768 | bytes 6144 | tf_op jit(solution)/shard_map/psum | solution.py:104
  405.3 0.7 copy.67
  405.9 0.1 copy.78
  406.0 27.2 %psum.22 = f32[4,36]{0,1:T(8,128)S(1)} all-reduce(f32[4,36]{0,1:T(8,128)S(1)} %multiply_bitcast_fusion), channel_id=1, replica_groups=mesh['ka'=8,'pb'=16,'row'=4] {'ka'}, use_global_device_ids=true, to_apply=%region_5.6 | all-reduce | flops 144 | bytes 1152 | tf_op jit(solution)/shard_map/psum | solution.py:103
  433.2 16.5 %psum.23 = f32[4,36]{0,1:T(8,128)S(1)} all-reduce(f32[4,36]{0,1:T(8,128)S(1)} %psum.22), channel_id=1, replica_groups=mesh['ka'=8,'pb'=16,'row'=4] {'row'}, use_global_device_ids=true, to_apply=%region_6.7 | all-reduce | flops 144 | bytes 1152 | tf_op jit(solution)/shard_map/psum | solution.py:103
  449.7 0.7 copy.68
  450.4 0.0 copy-done.1
  (17 shorter events, 0.2 us)
Async XLA Ops:
  7.2 3.7 copy-start
  7.2 175.7 %all-gather.4.cloned.1.call-start = ((), (), s32[]{:S(2)}) async-start(), calls=%async_computation | async-start | bytes 6488064 | tf_op jit(solution)/shard_map/all_gather | solution.py:73
  9.0 178.6 %all-gather.6.cloned.1.call-start = ((), (), s32[]{:S(2)}) async-start(), calls=%async_computation.1 | async-start | bytes 10948608 | tf_op jit(solution)/shard_map/all_gather | solution.py:82
  243.1 23.0 %copy-start.2 = (f32[4,36]{1,0:T(4,128)S(1)}, f32[4,36]{1,0:T(4,128)}, u32[]{:S(2)}) copy-start(f32[4,36]{1,0:T(4,128)} %param.11) | copy-start | bytes 1732
  266.1 184.3 %copy-start.1 = (s32[4,1024]{1,0:T(4,128)S(1)}, s32[4,1024]{1,0:T(4,128)}, u32[]{:S(2)}) copy-start(s32[4,1024]{1,0:T(4,128)} %param.15) | copy-start | bytes 49156
Sparse Core Ops, SparseCore 0:
  11.1 75.5 all-gather.3
  89.9 93.6 all-gather.5
